TPU v7x, 32 devices: a whole 2x2x4 slice. The times are simulated.
32 devices in a mesh: img: 8 (over z, y), txt: 4 (over x, core).
Axes of the slice: x: 2, y: 2, z: 4, core: 2. Of those that a mesh axis runs over, the one named last changes fastest.
Arguments:
- images: float32 [1024, 1024], P(('img', 'txt')), may hold values from -1 to 1
- texts: float32 [1024, 1024], P(('txt', 'img')), may hold values from -1 to 1
- labels: int32 [1024], P('img'), may hold values from 0 to 1023, each once
Outputs:
- row_loss: float32 [1024], P('img')
- image_grad: float32 [1024, 1024], P(('img', 'txt'))
- text_grad: float32 [1024, 1024], P(('txt', 'img'))
Inputs may be any that keep to these rules, and one draw needn't show every extreme that they name: `labels`: each text index appears exactly once.
All inputs are finite; a program needn't handle non-finite values.
Results may differ from a plain program's by a relative error of at most 0.017.
Values may be sent and summed in bfloat16 or wider, within the bound.
A program may use at most 64 MiB of HBM per device.

v0:
```python
import jax
import jax.numpy as jnp
from jax import lax
from jax.sharding import PartitionSpec as P

logit_scale = 100.0


def merged(part, axis, combine):
    gathered = jax.tree.map(lambda a: lax.all_gather(a, axis), part)

    def take(source):
        return jax.tree.map(lambda a: lax.dynamic_index_in_dim(a, source, 0, False), gathered)

    return lax.fori_loop(
        1, lax.axis_size(axis), lambda source, state: combine(state, take(source)), take(0)
    )


def combine(earlier, later):
    highest = jnp.maximum(earlier[0], later[0])
    total = earlier[1] * jnp.exp(earlier[0] - highest) + later[1] * jnp.exp(later[0] - highest)
    return (highest, total, earlier[2] + later[2])


def local(images, texts, labels):
    img_panel = lax.all_gather(images.astype(jnp.bfloat16), "txt", axis=0, tiled=True)
    txt_panel = lax.all_gather(texts.astype(jnp.bfloat16), "img", axis=0, tiled=True)
    text_rows = txt_panel.shape[0]
    logits = logit_scale * lax.dot_general(
        img_panel, txt_panel, (((1,), (1,)), ((), ())), preferred_element_type=jnp.float32
    )
    columns = lax.axis_index("txt") * text_rows + lax.broadcasted_iota(jnp.int32, (1, text_rows), 1)
    hits = columns == labels[:, None]
    highest = jnp.max(logits, axis=1)
    exp_total = jnp.sum(jnp.exp(logits - highest[:, None]), axis=1)
    positive = jnp.sum(jnp.where(hits, logits, 0.0), axis=1)
    highest, exp_total, positive = merged((highest, exp_total, positive), "txt", combine)
    log_total = highest + jnp.log(exp_total)
    row_loss = log_total - positive
    grad_tile = (
        logit_scale * (jnp.exp(logits - log_total[:, None]) - hits.astype(jnp.float32))
    ).astype(jnp.bfloat16)
    terms = jnp.dot(grad_tile, txt_panel, preferred_element_type=jnp.float32)
    image_grad = lax.psum_scatter(
        terms.astype(jnp.bfloat16), "txt", scatter_dimension=0, tiled=True
    ).astype(jnp.float32)
    terms = lax.dot_general(
        grad_tile, img_panel, (((0,), (0,)), ((), ())), preferred_element_type=jnp.float32
    )
    text_grad = lax.psum_scatter(
        terms.astype(jnp.bfloat16), "img", scatter_dimension=0, tiled=True
    ).astype(jnp.float32)
    return (row_loss, image_grad, text_grad)


def solution(mesh):
    in_specs = (P(("img", "txt"), None), P(("txt", "img"), None), P("img"))
    out_specs = (P("img"), P(("img", "txt"), None), P(("txt", "img"), None))
    return jax.shard_map(local, mesh=mesh, in_specs=in_specs, out_specs=out_specs, check_vma=False)
```

profile of v0, /device:TPU:0, one launch (start us, length us, event | category | flops | bytes accessed | tf_op | source)
XLA Modules:
  0.0 161.3 jit_solution(13547509192258138272)
XLA Ops:
  7.2 0.0 reduce-scatter.3.cloned.1.call-start
  7.2 0.9 convert_element_type.24
  8.1 0.0 copy-start
  8.1 7.4 %all_gather.24 = bf16[128,1024]{1,0:T(8,128)(2,1)S(1)} all-gather(bf16[32,1024]{1,0:T(8,128)(2,1)S(1)} %convert_element_type.24), channel_id=1, replica_groups=mesh['img'=8,'txt'=4] {'txt'}, dimensions={0}, use_global_device_ids=true | all-gather | bytes 327680 | tf_op jit(solution)/shard_map/all_gather | solution.py:27
  15.5 0.0 copy-done
  15.5 31.9 %all_gather.25 = bf16[256,1024]{1,0:T(8,128)(2,1)S(1)} all-gather(bf16[32,1024]{1,0:T(8,128)(2,1)S(1)} %convert_element_type.25), channel_id=1, replica_groups=mesh['img'=8,'txt'=4] {'img'}, dimensions={0}, use_global_device_ids=true | all-gather | bytes 589824 | tf_op jit(solution)/shard_map/all_gather | solution.py:28
  47.4 0.4 fusion.15
  47.8 5.1 %all-gather.3 = f32[4,1,128]{2,1,0:T(1,128)S(1)} all-gather(f32[1,1,128]{2,1,0:T(1,128)S(1)} %bitcast.38), channel_id=2, replica_groups=mesh['img'=8,'txt'=4] {'txt'}, dimensions={0}, use_global_device_ids=true | all-gather | bytes 2560 | tf_op jit(solution)/shard_map/all_gather | solution.py:10
  52.9 0.0 copy-start.1
  52.9 0.7 copy-done.1
  53.6 0.2 fusion.7
  53.7 5.1 %all-gather.4 = f32[4,1,128]{2,1,0:T(1,128)S(1)} all-gather(f32[1,1,128]{2,1,0:T(1,128)S(1)} %bitcast.40), channel_id=3, replica_groups=mesh['img'=8,'txt'=4] {'txt'}, dimensions={0}, use_global_device_ids=true | all-gather | bytes 2560 | tf_op jit(solution)/shard_map/all_gather | solution.py:10
  58.8 5.0 %all-gather.5 = f32[4,1,128]{2,1,0:T(1,128)S(1)} all-gather(f32[1,1,128]{2,1,0:T(1,128)S(1)} %bitcast.39), channel_id=4, replica_groups=mesh['img'=8,'txt'=4] {'txt'}, dimensions={0}, use_global_device_ids=true | all-gather | bytes 2560 | tf_op jit(solution)/shard_map/all_gather | solution.py:10
  63.9 0.1 while.19
  64.0 0.5 fusion.14
  64.5 1.0 convolution_convert_fusion.1
  65.5 0.0 reduce-scatter.3.cloned.1.call-update
  65.5 0.0 reduce-scatter.5.cloned.1.call-start
  65.6 1.2 convolution_convert_fusion
  66.8 0.0 reduce-scatter.5.cloned.1.call-update
  66.8 19.7 %reduce-scatter.3.cloned.1.call-done = bf16[32,1024]{1,0:T(8,128)(2,1)} async-done(((bf16[128,1024]{1,0:T(8,128)(2,1)}), bf16[32,1024]{1,0:T(8,128)(2,1)}) %reduce-scatter.3.cloned.1.call-update) | async-done | bytes 65552 | tf_op jit(solution)/shard_map/reduce_scatter | solution.py:45
  86.5 1.5 convert_element_type.29
  88.0 65.0 %reduce-scatter.5.cloned.1.call-done = bf16[32,1024]{1,0:T(8,128)(2,1)} async-done(((bf16[256,1024]{1,0:T(8,128)(2,1)}), bf16[32,1024]{1,0:T(8,128)(2,1)}) %reduce-scatter.5.cloned.1.call-update) | async-done | bytes 65552 | tf_op jit(solution)/shard_map/reduce_scatter | solution.py:51
  152.9 1.5 convert_element_type.31
  (8 shorter events, 0.1 us)
Async XLA Ops:
  7.2 79.3 %reduce-scatter.3.cloned.1.call-start = ((), (), s32[]{:S(2)}) async-start(), calls=%async_computation.2 | async-start | bytes 327680 | tf_op jit(solution)/shard_map/reduce_scatter | solution.py:45
  8.1 7.4 %copy-start = (f32[32,1024]{1,0:T(8,128)S(1)}, f32[32,1024]{1,0:T(8,128)}, u32[]{:S(2)}) copy-start(f32[32,1024]{1,0:T(8,128)} %param.6) | copy-start | bytes 393220
  52.9 0.7 copy-start.1
  65.5 87.4 %reduce-scatter.5.cloned.1.call-start = ((), (), s32[]{:S(2)}) async-start(), calls=%async_computation.3 | async-start | bytes 589824 | tf_op jit(solution)/shard_map/reduce_scatter | solution.py:51
Sparse Core Ops, SparseCore 0:
  65.6 20.7 reduce-scatter.2
  89.8 63.0 reduce-scatter.4
where the time goes:
time: 162 us; the launch traced here: 161 us
  waiting for transfers between devices  84.7 us (52%)
  blocking collectives  54.5 us (34%)
  between operations  14.1 us (9%)
  other arithmetic  4.71 us (3%)
  matrix products  2.58 us (2%)
    reduce_scatter x1, waiting for transfers between devices, local(): lax.psum_scatter(terms.astype(jnp.bfloat16), 'img', scatter_dimension=0,...  65 us
    all_gather x1, blocking collectives, local(): lax.all_gather(texts.astype(jnp.bfloat16), 'img', axis=0, tiled=True)  31.9 us
    reduce_scatter x1, waiting for transfers between devices, local(): lax.psum_scatter(terms.astype(jnp.bfloat16), 'txt', scatter_dimension=0,...  19.7 us
    all_gather x3, blocking collectives, merged(): gathered = jax.tree.map(lambda a: lax.all_gather(a, axis), part)  15.2 us
    all_gather x1, blocking collectives, local(): lax.all_gather(images.astype(jnp.bfloat16), 'txt', axis=0, tiled=True)  7.35 us
  transfers between devices with their start and end apart: 2, of which 2 were waited for; matrix products, arithmetic and copies ran while one was open for 2% of the time, Pallas kernels for 0%

commit v1 on v0

--- a/solution.py
+++ b/solution.py
@@ -25,7 +25,17 @@
 
 def local(images, texts, labels):
     img_panel = lax.all_gather(images.astype(jnp.bfloat16), "txt", axis=0, tiled=True)
-    txt_panel = lax.all_gather(texts.astype(jnp.bfloat16), "img", axis=0, tiled=True)
+    shard = texts.astype(jnp.bfloat16)
+    ways = lax.axis_size("img")
+    up = [(d, (d + 1) % ways) for d in range(ways)]
+    down = [(d, (d - 1) % ways) for d in range(ways)]
+    earlier_2, later_2 = ([shard], [shard])
+    for _ in range(ways // 2):
+        earlier_2.append(lax.ppermute(earlier_2[-1], "img", up))
+    for _ in range((ways - 1) // 2):
+        later_2.append(lax.ppermute(later_2[-1], "img", down))
+    line = jnp.concatenate([*earlier_2[::-1], *later_2[1:]], axis=0)
+    txt_panel = jnp.roll(line, (lax.axis_index("img") - ways // 2) * shard.shape[0], axis=0)
     text_rows = txt_panel.shape[0]
     logits = logit_scale * lax.dot_general(
         img_panel, txt_panel, (((1,), (1,)), ((), ())), preferred_element_type=jnp.float32

time: 162 us -> 158 us (0.975)
  blocking collectives: 54.5 us -> 21 us
  starting transfers between devices: 0.08 us -> 17.3 us
  waiting for transfers between devices: 84.7 us -> 96.1 us
    all_gather x1 -> x0, blocking collectives: 31.9 us -> none  [local(): lax.all_gather(texts.astype(jnp.bfloat16), 'img', axis=0, tiled=True)]
    ppermute x0 -> x7, starting transfers between devices: none -> 17.2 us  [the longest x3 14.2 us: local(): later_2.append(lax.ppermute(later_2[-1], 'img', down))]
    ppermute x0 -> x7, waiting for transfers between devices: none -> 10.7 us  [the longest x4 9.73 us: local(): earlier_2.append(lax.ppermute(earlier_2[-1], 'img', up))]
  transfers between devices with their start and end apart: 2 -> 9, of which waited for: 2 -> 6; matrix products, arithmetic and copies ran while one was open for 2% -> 2% of each run, Pallas kernels for 0% -> 0%
where the time goes in v1:
time: 158 us; the launch traced here: 157 us
  waiting for transfers between devices  96.1 us (61%)
  blocking collectives  21 us (13%)
  starting transfers between devices  17.3 us (11%)
  between operations  14.2 us (9%)
  other arithmetic  4.7 us (3%)
  matrix products  2.5 us (2%)
  local copies, waits for them, and re-layouts  1.63 us (1%)
    reduce_scatter x1, waiting for transfers between devices, local(): lax.psum_scatter(terms.astype(jnp.bfloat16), 'img', scatter_dimension=0,...  64.5 us
    reduce_scatter x1, waiting for transfers between devices, local(): lax.psum_scatter(terms.astype(jnp.bfloat16), 'txt', scatter_dimension=0,...  20.9 us
    all_gather x3, blocking collectives, merged(): gathered = jax.tree.map(lambda a: lax.all_gather(a, axis), part)  15.1 us
    ppermute x3, starting transfers between devices, local(): later_2.append(lax.ppermute(later_2[-1], 'img', down))  14.2 us
    ppermute x4, waiting for transfers between devices, local(): earlier_2.append(lax.ppermute(earlier_2[-1], 'img', up))  9.73 us
    all_gather x1, blocking collectives, local(): lax.all_gather(images.astype(jnp.bfloat16), 'txt', axis=0, tiled=True)  5.89 us
  transfers between devices with their start and end apart: 9, of which 6 were waited for; matrix products, arithmetic and copies ran while one was open for 2% of the time, Pallas kernels for 0%

profile of v1, /device:TPU:0, one launch (start us, length us, event | category | flops | bytes accessed | tf_op | source)
XLA Modules:
  0.0 157.5 jit_solution(17834609707366996570)
XLA Ops:
  7.2 0.0 reduce-scatter.3.cloned.1.call-start
  7.2 0.9 convert_element_type.24
  8.2 3.0 %collective-permute-start = (bf16[32,1024]{1,0:T(8,128)(2,1)S(1)}, bf16[32,1024]{1,0:T(8,128)(2,1)S(1)}, u32[]{:S(2)}, u32[]{:S(2)}) collective-permute-start(bf16[32,1024]{1,0:T(8,128)(2,1)S(1)} %convert_element_type.24), channel_id=1, source_target_pairs={{0,4},{4,8},{8,12},{12,16},{16,20},{20,24},{24,28},{28,0},{1,5},{5... | collective-permute-start | bytes 196616 | tf_op jit(solution)/shard_map/ppermute | solution.py:34
  11.2 5.3 %collective-permute-done = bf16[32,1024]{1,0:T(8,128)(2,1)S(1)} collective-permute-done((bf16[32,1024]{1,0:T(8,128)(2,1)S(1)}, bf16[32,1024]{1,0:T(8,128)(2,1)S(1)}, u32[]{:S(2)}, u32[]{:S(2)}) %collective-permute-start) | collective-permute-done | bytes 65568 | tf_op jit(solution)/shard_map/ppermute | solution.py:34
  16.5 4.7 %collective-permute-start.4 = (bf16[32,1024]{1,0:T(8,128)(2,1)S(1)}, bf16[32,1024]{1,0:T(8,128)(2,1)S(1)}, u32[]{:S(2)}, u32[]{:S(2)}) collective-permute-start(bf16[32,1024]{1,0:T(8,128)(2,1)S(1)} %convert_element_type.24), channel_id=1, source_target_pairs={{0,28},{4,0},{8,4},{12,8},{16,12},{20,16},{24,20},{28,24},{1,29},{... | collective-permute-start | bytes 196616 | tf_op jit(solution)/shard_map/ppermute | solution.py:36
  21.2 2.2 %collective-permute-done.1 = bf16[32,1024]{1,0:T(8,128)(2,1)S(1)} collective-permute-done((bf16[32,1024]{1,0:T(8,128)(2,1)S(1)}, bf16[32,1024]{1,0:T(8,128)(2,1)S(1)}, u32[]{:S(2)}, u32[]{:S(2)}) %collective-permute-start.1) | collective-permute-done | bytes 65568 | tf_op jit(solution)/shard_map/ppermute | solution.py:34
  23.5 4.7 %collective-permute-start.5 = (bf16[32,1024]{1,0:T(8,128)(2,1)S(1)}, bf16[32,1024]{1,0:T(8,128)(2,1)S(1)}, u32[]{:S(2)}, u32[]{:S(2)}) collective-permute-start(bf16[32,1024]{1,0:T(8,128)(2,1)S(1)} %collective-permute-done.4), channel_id=1, source_target_pairs={{0,28},{4,0},{8,4},{12,8},{16,12},{20,16},{24,20},{28,24},{1,29},{... | collective-permute-start | bytes 196616 | tf_op jit(solution)/shard_map/ppermute | solution.py:36
  28.2 2.2 %collective-permute-done.2 = bf16[32,1024]{1,0:T(8,128)(2,1)S(1)} collective-permute-done((bf16[32,1024]{1,0:T(8,128)(2,1)S(1)}, bf16[32,1024]{1,0:T(8,128)(2,1)S(1)}, u32[]{:S(2)}, u32[]{:S(2)}) %collective-permute-start.2) | collective-permute-done | bytes 65568 | tf_op jit(solution)/shard_map/ppermute | solution.py:34
  30.4 5.9 %all_gather.21 = bf16[128,1024]{1,0:T(8,128)(2,1)S(1)} all-gather(bf16[32,1024]{1,0:T(8,128)(2,1)S(1)} %convert_element_type.25), channel_id=1, replica_groups=mesh['img'=8,'txt'=4] {'txt'}, dimensions={0}, use_global_device_ids=true | all-gather | bytes 327680 | tf_op jit(solution)/shard_map/all_gather | solution.py:27
  36.3 0.0 collective-permute-done.5
  36.3 4.7 %collective-permute-start.6 = (bf16[32,1024]{1,0:T(8,128)(2,1)S(1)}, bf16[32,1024]{1,0:T(8,128)(2,1)S(1)}, u32[]{:S(2)}, u32[]{:S(2)}) collective-permute-start(bf16[32,1024]{1,0:T(8,128)(2,1)S(1)} %collective-permute-done.5), channel_id=1, source_target_pairs={{0,28},{4,0},{8,4},{12,8},{16,12},{20,16},{24,20},{28,24},{1,29},{... | collective-permute-start | bytes 196616 | tf_op jit(solution)/shard_map/ppermute | solution.py:36
  41.1 0.0 copy-start
  41.1 0.9 copy-done
  42.0 0.9 collective-permute-done.6
  43.1 0.3 fusion.22
  43.4 0.0 copy-start.2
  43.4 0.7 copy-done.2
  44.0 0.1 fusion.9
  44.2 5.1 %all-gather.5 = f32[4,1,128]{2,1,0:T(1,128)S(1)} all-gather(f32[1,1,128]{2,1,0:T(1,128)S(1)} %bitcast.52), channel_id=4, replica_groups=mesh['img'=8,'txt'=4] {'txt'}, dimensions={0}, use_global_device_ids=true | all-gather | bytes 2560 | tf_op jit(solution)/shard_map/all_gather | solution.py:10
  49.2 5.0 %all-gather.4 = f32[4,1,128]{2,1,0:T(1,128)S(1)} all-gather(f32[1,1,128]{2,1,0:T(1,128)S(1)} %bitcast.51), channel_id=3, replica_groups=mesh['img'=8,'txt'=4] {'txt'}, dimensions={0}, use_global_device_ids=true | all-gather | bytes 2560 | tf_op jit(solution)/shard_map/all_gather | solution.py:10
  54.3 5.0 %all-gather.3 = f32[4,1,128]{2,1,0:T(1,128)S(1)} all-gather(f32[1,1,128]{2,1,0:T(1,128)S(1)} %bitcast.50), channel_id=2, replica_groups=mesh['img'=8,'txt'=4] {'txt'}, dimensions={0}, use_global_device_ids=true | all-gather | bytes 2560 | tf_op jit(solution)/shard_map/all_gather | solution.py:10
  59.3 0.1 while.19
  59.4 0.5 fusion.21
  60.0 1.0 convolution_convert_fusion.1
  61.0 0.0 reduce-scatter.3.cloned.1.call-update
  61.0 0.0 reduce-scatter.5.cloned.1.call-start
  61.1 1.1 convolution_convert_fusion
  62.2 0.0 reduce-scatter.5.cloned.1.call-update
  62.2 20.9 %reduce-scatter.3.cloned.1.call-done = bf16[32,1024]{1,0:T(8,128)(2,1)} async-done(((bf16[128,1024]{1,0:T(8,128)(2,1)}), bf16[32,1024]{1,0:T(8,128)(2,1)}) %reduce-scatter.3.cloned.1.call-update) | async-done | bytes 65552 | tf_op jit(solution)/shard_map/reduce_scatter | solution.py:55
  83.1 1.5 convert_element_type.29
  84.6 64.5 %reduce-scatter.5.cloned.1.call-done = bf16[32,1024]{1,0:T(8,128)(2,1)} async-done(((bf16[256,1024]{1,0:T(8,128)(2,1)}), bf16[32,1024]{1,0:T(8,128)(2,1)}) %reduce-scatter.5.cloned.1.call-update) | async-done | bytes 65552 | tf_op jit(solution)/shard_map/reduce_scatter | solution.py:61
  149.1 1.5 convert_element_type.31
  (31 shorter events, 0.2 us)
Async XLA Ops:
  7.2 14.1 %copy-start.1 = (f32[32,1024]{1,0:T(8,128)S(1)}, f32[32,1024]{1,0:T(8,128)}, u32[]{:S(2)}) copy-start(f32[32,1024]{1,0:T(8,128)} %param.5) | copy-start | bytes 393220
  7.2 75.9 %reduce-scatter.3.cloned.1.call-start = ((), (), s32[]{:S(2)}) async-start(), calls=%async_computation.2 | async-start | bytes 327680 | tf_op jit(solution)/shard_map/reduce_scatter | solution.py:55
  8.2 8.3 %collective-permute-start = (bf16[32,1024]{1,0:T(8,128)(2,1)S(1)}, bf16[32,1024]{1,0:T(8,128)(2,1)S(1)}, u32[]{:S(2)}, u32[]{:S(2)}) collective-permute-start(bf16[32,1024]{1,0:T(8,128)(2,1)S(1)} %convert_element_type.24), channel_id=1, source_target_pairs={{0,4},{4,8},{8,12},{12,16},{16,20},{20,24},{24,28},{28,0},{1,5},{5... | collective-permute-start | bytes 196616 | tf_op jit(solution)/shard_map/ppermute | solution.py:34
  16.5 7.0 %collective-permute-start.1 = (bf16[32,1024]{1,0:T(8,128)(2,1)S(1)}, bf16[32,1024]{1,0:T(8,128)(2,1)S(1)}, u32[]{:S(2)}, u32[]{:S(2)}) collective-permute-start(bf16[32,1024]{1,0:T(8,128)(2,1)S(1)} %collective-permute-done), channel_id=1, source_target_pairs={{0,4},{4,8},{8,12},{12,16},{16,20},{20,24},{24,28},{28,0},{1,5},{5... | collective-permute-start | bytes 196616 | tf_op jit(solution)/shard_map/ppermute | solution.py:34
  16.5 7.0 %collective-permute-start.4 = (bf16[32,1024]{1,0:T(8,128)(2,1)S(1)}, bf16[32,1024]{1,0:T(8,128)(2,1)S(1)}, u32[]{:S(2)}, u32[]{:S(2)}) collective-permute-start(bf16[32,1024]{1,0:T(8,128)(2,1)S(1)} %convert_element_type.24), channel_id=1, source_target_pairs={{0,28},{4,0},{8,4},{12,8},{16,12},{20,16},{24,20},{28,24},{1,29},{... | collective-permute-start | bytes 196616 | tf_op jit(solution)/shard_map/ppermute | solution.py:36
  23.5 7.0 %collective-permute-start.2 = (bf16[32,1024]{1,0:T(8,128)(2,1)S(1)}, bf16[32,1024]{1,0:T(8,128)(2,1)S(1)}, u32[]{:S(2)}, u32[]{:S(2)}) collective-permute-start(bf16[32,1024]{1,0:T(8,128)(2,1)S(1)} %collective-permute-done.1), channel_id=1, source_target_pairs={{0,4},{4,8},{8,12},{12,16},{16,20},{20,24},{24,28},{28,0},{1,5},{5... | collective-permute-start | bytes 196616 | tf_op jit(solution)/shard_map/ppermute | solution.py:34
  23.5 12.8 %collective-permute-start.5 = (bf16[32,1024]{1,0:T(8,128)(2,1)S(1)}, bf16[32,1024]{1,0:T(8,128)(2,1)S(1)}, u32[]{:S(2)}, u32[]{:S(2)}) collective-permute-start(bf16[32,1024]{1,0:T(8,128)(2,1)S(1)} %collective-permute-done.4), channel_id=1, source_target_pairs={{0,28},{4,0},{8,4},{12,8},{16,12},{20,16},{24,20},{28,24},{1,29},{... | collective-permute-start | bytes 196616 | tf_op jit(solution)/shard_map/ppermute | solution.py:36
  30.4 10.6 %collective-permute-start.3 = (bf16[32,1024]{1,0:T(8,128)(2,1)S(1)}, bf16[32,1024]{1,0:T(8,128)(2,1)S(1)}, u32[]{:S(2)}, u32[]{:S(2)}) collective-permute-start(bf16[32,1024]{1,0:T(8,128)(2,1)S(1)} %collective-permute-done.2), channel_id=1, source_target_pairs={{0,4},{4,8},{8,12},{12,16},{16,20},{20,24},{24,28},{28,0},{1,5},{5... | collective-permute-start | bytes 196616 | tf_op jit(solution)/shard_map/ppermute | solution.py:34
  36.3 6.6 %collective-permute-start.6 = (bf16[32,1024]{1,0:T(8,128)(2,1)S(1)}, bf16[32,1024]{1,0:T(8,128)(2,1)S(1)}, u32[]{:S(2)}, u32[]{:S(2)}) collective-permute-start(bf16[32,1024]{1,0:T(8,128)(2,1)S(1)} %collective-permute-done.5), channel_id=1, source_target_pairs={{0,28},{4,0},{8,4},{12,8},{16,12},{20,16},{24,20},{28,24},{1,29},{... | collective-permute-start | bytes 196616 | tf_op jit(solution)/shard_map/ppermute | solution.py:36
  41.1 0.9 copy-start
  43.4 0.7 copy-start.2
  61.0 88.1 %reduce-scatter.5.cloned.1.call-start = ((), (), s32[]{:S(2)}) async-start(), calls=%async_computation.3 | async-start | bytes 589824 | tf_op jit(solution)/shard_map/reduce_scatter | solution.py:61
Sparse Core Ops, SparseCore 0:
  61.1 21.9 reduce-scatter.2
  86.4 62.6 reduce-scatter.4
